TPU v7x, 32 devices: a whole 2x2x4 slice. The times are simulated.
32 devices in a mesh: segment: 4 (over y, core), chan: 4 (over z), tm: 2 (over x).
Axes of the slice: x: 2, y: 2, z: 4, core: 2. Of those that a mesh axis runs over, the one named last changes fastest.
Arguments:
- voltages: bfloat16 [3, 512, 2048, 128], P(None, 'chan', ('segment', 'tm')), may hold values from -6 to 6
- flags: int32 [512], P('chan'), may hold values 0 or 1
- delays: int32 [512, 512], replicated, may hold values from 0 to 127
- analysis_taps: float32 [4, 64], replicated, may hold values from -3 to 3
- synthesis_taps: float32 [4, 64], replicated, may hold values from -3 to 3
Outputs:
- vis: float32 [64, 8, 2, 512, 512], P('chan', ('segment', 'tm'))
- beams: bfloat16 [3, 512, 2048, 128], P(None, 'chan', ('segment', 'tm'))
All inputs are finite; a program needn't handle non-finite values. No bound on the sum of `flags` on one device may be relied on, other than what follows from the above.
Results may differ from a plain program's by a relative error of at most 0.008.
Values may be sent and summed in bfloat16 or wider, within the bound.
A program may use at most 256 MiB of HBM per device.

v0:
```python
import math

import jax
import jax.numpy as jnp
from jax import lax
from jax.sharding import PartitionSpec as P

A = 512
C = 64
TAPS = 4
FB = 256
MB = 3


def shifted(value, axis, steps):
    count = lax.axis_size(axis)
    leading, last = (max(0, -steps), min(count, count - steps))
    return lax.ppermute(value, axis, [(source, source + steps) for source in range(leading, last)])


def forward_table(chan_count):
    indices = jnp.arange(2 * chan_count, dtype=jnp.int32)
    out_chan = indices // 2
    out_part = indices % 2
    in_part = indices // chan_count
    in_sample = indices % chan_count
    wrapped = out_chan[:, None] * in_sample[None, :] % chan_count
    angles = wrapped.astype(jnp.float32) * (2.0 * math.pi / chan_count)
    cosine = jnp.cos(angles)
    sine_part = jnp.sin(angles)
    real_row = jnp.where(in_part[None, :] == 0, cosine, sine_part)
    imag_row = jnp.where(in_part[None, :] == 0, -sine_part, cosine)
    dft_table = jnp.where(out_part[:, None] == 0, real_row, imag_row)
    return (dft_table * (1.0 / math.sqrt(chan_count))).astype(jnp.bfloat16)


def inverse_table(chan_count):
    indices = jnp.arange(2 * chan_count, dtype=jnp.int32)
    out_part = indices // chan_count
    out_sample = indices % chan_count
    in_chan = indices // 2
    in_part = indices % 2
    wrapped = out_sample[:, None] * in_chan[None, :] % chan_count
    angles = wrapped.astype(jnp.float32) * (2.0 * math.pi / chan_count)
    cosine = jnp.cos(angles)
    sine_part = jnp.sin(angles)
    real_row = jnp.where(in_part[None, :] == 0, cosine, -sine_part)
    imag_row = jnp.where(in_part[None, :] == 0, sine_part, cosine)
    dft_table = jnp.where(out_part[:, None] == 0, real_row, imag_row)
    return (dft_table * (1.0 / math.sqrt(chan_count))).astype(jnp.bfloat16)


def steering_weights(delays, channel_list, chan_count):
    odd_steps = 2 * channel_list + 1
    wrapped = odd_steps[:, None, None] * delays[None, :, :] % (2 * chan_count)
    angles = wrapped.astype(jnp.float32) * (math.pi / chan_count)
    cosine = jnp.swapaxes(jnp.cos(angles), 1, 2)
    sine_part = jnp.swapaxes(jnp.sin(angles), 1, 2)
    upper = jnp.concatenate([cosine, sine_part], axis=2)
    lower = jnp.concatenate([-sine_part, cosine], axis=2)
    return jnp.concatenate([upper, lower], axis=1).astype(jnp.bfloat16)


def channelize(block, rim, paired_filter_taps, forward, flag_scale):
    history = paired_filter_taps.shape[0] - 1
    frames = block.shape[1]
    padded = jnp.concatenate([rim.astype(jnp.float32), block.astype(jnp.float32)], axis=1)
    weighted = paired_filter_taps[0] * padded[:, history : history + frames]
    for tap_number in range(1, history + 1):
        weighted = (
            weighted
            + paired_filter_taps[tap_number]
            * padded[:, history - tap_number : history - tap_number + frames]
        )
    weighted = weighted.astype(jnp.bfloat16)
    spectra = jnp.einsum("oi,afi->oaf", forward, weighted, preferred_element_type=jnp.float32)
    spectra = spectra * flag_scale[None, :, None]
    return spectra.astype(jnp.bfloat16).reshape(forward.shape[0] // 2, 2, block.shape[0], frames)


def gram_block(turned):
    left_part = jnp.concatenate([turned[:, 0], turned[:, 1]], axis=-1)
    rotated = jnp.concatenate([turned[:, 1], -turned[:, 0]], axis=-1)
    stacked = jnp.concatenate([left_part, rotated], axis=1)
    return jnp.einsum("cif,cjf->cij", stacked, left_part, preferred_element_type=jnp.float32)


def form_beams(turned, steering_matrix):
    chan_local, parts, antennas, frames = turned.shape
    flattened_rows = turned.reshape(chan_local, parts * antennas, frames)
    formed_beams = jnp.einsum(
        "goq,gqk->gok", steering_matrix, flattened_rows, preferred_element_type=jnp.float32
    )
    formed_beams = (formed_beams * (1.0 / math.sqrt(antennas))).astype(jnp.bfloat16)
    return formed_beams.reshape(chan_local, 2, steering_matrix.shape[1] // 2, frames)


def tail_frames(inverse_part, count, history):
    beam_local, frames, width_both = inverse_part.shape
    block_frames = frames // count
    blocks = inverse_part.reshape(beam_local, count, block_frames, width_both)
    return blocks[:, :, block_frames - history :, :]


def synthesize(inverse_part, tails, count, paired_filter_taps):
    history = paired_filter_taps.shape[0] - 1
    beam_local, frames, width_both = inverse_part.shape
    block_frames = frames // count
    blocks = inverse_part.reshape(beam_local, count, block_frames, width_both)
    padded = jnp.concatenate([tails.astype(jnp.float32), blocks.astype(jnp.float32)], axis=2)
    weighted = paired_filter_taps[0] * padded[:, :, history : history + block_frames]
    for tap_number in range(1, history + 1):
        weighted = (
            weighted
            + paired_filter_taps[tap_number]
            * padded[:, :, history - tap_number : history - tap_number + block_frames]
        )
    return jnp.transpose(weighted.astype(jnp.bfloat16), (1, 0, 2, 3))


def per_device(voltages, flags, delays, analysis_taps, synthesis_taps):
    chan_local = C // lax.axis_size("chan")
    history = TAPS - 1
    forward = forward_table(C)
    inverse_result = inverse_table(C)
    analysis_both = jnp.concatenate([analysis_taps, analysis_taps], axis=1)
    synthesis_both = jnp.concatenate([synthesis_taps, synthesis_taps], axis=1)
    flag_scale = flags.astype(jnp.float32)
    channel_list = lax.axis_index("chan") * chan_local + jnp.arange(chan_local, dtype=jnp.int32)
    steering_matrix = steering_weights(delays, channel_list, C)
    rims_all = shifted(voltages[:, :, FB - history :, :], ("segment", "tm"), 1)
    rim_list = [rims_all[batch_step] for batch_step in range(MB)]
    spectra_list = [
        channelize(voltages[batch_step], rim_list[batch_step], analysis_both, forward, flag_scale)
        for batch_step in range(MB)
    ]
    gram_total = None
    beam_list = []
    for batch_step in range(MB):
        turned = lax.all_to_all(
            spectra_list[batch_step], "chan", split_axis=0, concat_axis=2, tiled=True
        )
        gram_piece = gram_block(turned)
        gram_total = gram_piece if batch_step == 0 else gram_total + gram_piece
        piece = lax.all_to_all(
            form_beams(turned, steering_matrix), "chan", split_axis=2, concat_axis=0, tiled=True
        )
        chan_all, parts, beam_local, frames = piece.shape
        flattened_rows = piece.reshape(chan_all * parts, beam_local, frames)
        result = jnp.einsum(
            "oi,ibf->bfo", inverse_result, flattened_rows, preferred_element_type=jnp.float32
        )
        inverse_single = result.astype(jnp.bfloat16)
        tails = shifted(tail_frames(inverse_single, 1, history), ("segment", "tm"), 1)
        beam_list.append(synthesize(inverse_single, tails, 1, synthesis_both))
    beams = jnp.concatenate(beam_list, axis=0)
    vis = (gram_total * (1.0 / (MB * FB))).reshape(chan_local, 1, 2, A, A)
    return (vis, beams)


def solution(mesh):
    placed = (P(None, "chan", ("segment", "tm"), None), P("chan"), P(), P(), P())
    return jax.shard_map(
        per_device,
        mesh=mesh,
        in_specs=placed,
        out_specs=(
            P("chan", ("segment", "tm"), None, None, None),
            P(None, "chan", ("segment", "tm"), None),
        ),
        check_vma=False,
    )
```

profile of v0, /device:TPU:0, one launch (start us, length us, event | category | flops | bytes accessed | tf_op | source)
XLA Modules:
  0.0 1388.2 jit_solution(14261170279806623218)
XLA Ops:
  0.6 1.3 slice.151
  2.0 4.9 collective-permute-start
  7.0 23.4 %bitcast_convert_fusion = (f32[128,256,128]{2,1,0:T(8,128)}, f32[128,256,128]{2,1,0:T(8,128)}, f32[128,256,128]{2,1,0:T(8,128)}) fusion(bf16[3,128,256,128]{3,2,1,0:T(8,128)(2,1)} %param.5), kind=kLoop, calls=%fused_computation.133 | loop fusion | flops 12582912 | bytes 75497472 | tf_op jit(solution)/shard_map/convert_element_type | solution.py:67
  30.7 32.0 %multiply_convert_fusion.3 = bf16[128,128,256]{2,0,1:T(8,128)(2,1)} fusion(f32[128]{0:T(128)S(1)} %convert_element_type.152, f32[128,3,128]{2,1,0:T(4,128)S(1)} %copy.50, f32[128,256,128]{2,1,0:T(8,128)} %get-tuple-element.10, f32[128]{0:T(128)S(1)} %get-tuple-element.33, f32[128]{0:T(128)S(1)} %get-tuple-element.34, f32[128]{0:T(128)S(1)} %get-tuple-element.35, ...), kind=kOutput, calls=%fused_computation.121 | convolution fusion | flops 1128595456 | bytes 25366272 | tf_op jit(solution)/shard_map/oi,afi->oaf/dot_general | solution.py:76
  62.7 13.1 reshape.197
  75.8 8.1 copy.51
  83.9 5.6 all-to-all-start.2
  89.7 32.3 %multiply_convert_fusion.4 = bf16[128,128,256]{2,0,1:T(8,128)(2,1)} fusion(f32[128]{0:T(128)S(1)} %convert_element_type.152, f32[128,3,128]{2,1,0:T(4,128)S(1)} %copy.47, f32[128,256,128]{2,1,0:T(8,128)} %get-tuple-element.12, f32[128]{0:T(128)S(1)} %get-tuple-element.33, f32[128]{0:T(128)S(1)} %get-tuple-element.34, f32[128]{0:T(128)S(1)} %get-tuple-element.35, ...), kind=kOutput, calls=%fused_computation.122 | convolution fusion | flops 1128595456 | bytes 25366272 | tf_op jit(solution)/shard_map/oi,afi->oaf/dot_general | solution.py:76
  122.0 13.1 reshape.196
  135.1 8.2 copy.48
  143.3 129.3 %all-to-all-done.2 = bf16[64,2,128,256]{3,1,2,0:T(2,128)(2,1)} async-done(((bf16[64,2,128,256]{3,1,2,0:T(2,128)(2,1)}), bf16[64,2,128,256]{3,1,2,0:T(2,128)(2,1)}, u32[]{:S(2)}, u32[]{:S(2)}) %all-to-all-start.2) | async-done | bytes 8388640 | tf_op jit(solution)/shard_map/all_to_all | solution.py:140
  272.6 5.8 all-to-all-start.1
  278.6 31.9 %multiply_convert_fusion.5 = bf16[128,128,256]{2,0,1:T(8,128)(2,1)} fusion(f32[128]{0:T(128)S(1)} %convert_element_type.152, f32[128,3,128]{2,1,0:T(4,128)S(1)} %copy.44, f32[128,256,128]{2,1,0:T(8,128)} %get-tuple-element.11, f32[128]{0:T(128)S(1)} %get-tuple-element.33, f32[128]{0:T(128)S(1)} %get-tuple-element.34, f32[128]{0:T(128)S(1)} %get-tuple-element.35, ...), kind=kOutput, calls=%fused_computation.123 | convolution fusion | flops 1128595456 | bytes 25366272 | tf_op jit(solution)/shard_map/oi,afi->oaf/dot_general | solution.py:76
  310.5 13.1 reshape.195
  323.5 8.2 copy.45
  331.7 129.2 %all-to-all-done.1 = bf16[64,2,128,256]{3,1,2,0:T(2,128)(2,1)} async-done(((bf16[64,2,128,256]{3,1,2,0:T(2,128)(2,1)}), bf16[64,2,128,256]{3,1,2,0:T(2,128)(2,1)}, u32[]{:S(2)}, u32[]{:S(2)}) %all-to-all-start.1) | async-done | bytes 8388640 | tf_op jit(solution)/shard_map/all_to_all | solution.py:140
  461.0 5.7 all-to-all-start
  467.0 70.0 %fusion.102 = (bf16[16,512,512]{2,1,0:T(8,128)(2,1)}, bf16[16,512,512]{2,1,0:T(8,128)(2,1)}, bf16[16,512,512]{2,1,0:T(8,128)(2,1)}) fusion(s32[512,512]{1,0:T(8,128)S(1)} %copy.53, s32[16]{0:T(128)S(1)} %multiply_add_fusion), kind=kLoop, calls=%fused_computation.143 | loop fusion | flops 75497472 | bytes 26214464 | tf_op jit(solution)/shard_map/convert.11
  537.0 8.5 copy.71
  545.5 21.3 %multiply_convert_fusion.1 = bf16[16,1024,256]{2,1,0:T(8,128)(2,1)} fusion(bf16[16,1024,256]{2,1,0:T(8,128)(2,1)} %bitcast.191, bf16[16,512,512]{2,1,0:T(8,128)(2,1)} %get-tuple-element.21, bf16[16,512,512]{2,1,0:T(8,128)(2,1)} %get-tuple-element.20, bf16[16,512,512]{2,1,0:T(8,128)(2,1)} %get-tuple-element.19), kind=kOutput, calls=%fused_computation.117 | convolution fusion | flops 8732540928 | bytes 41943040 | tf_op jit(solution)/shard_map/goq,gqk->gok/dot_general | solution.py:91
  566.8 16.5 %copy.60 = bf16[16,2,512,256]{3,1,0,2:T(2,128)(2,1)} copy(bf16[16,2,512,256]{3,2,1,0:T(8,128)(2,1)} %bitcast.192) | data formatting | bytes 16777216 | tf_op jit(solution)/shard_map/reshape | solution.py:95
  583.3 66.0 %all-to-all-done = bf16[64,2,128,256]{3,1,2,0:T(2,128)(2,1)} async-done(((bf16[64,2,128,256]{3,1,2,0:T(2,128)(2,1)}), bf16[64,2,128,256]{3,1,2,0:T(2,128)(2,1)}, u32[]{:S(2)}, u32[]{:S(2)}) %all-to-all-start) | async-done | bytes 8388640 | tf_op jit(solution)/shard_map/all_to_all | solution.py:140
  649.3 6.0 all-to-all-start.4
  655.3 8.5 copy.70
  663.8 21.3 %multiply_convert_fusion.2 = bf16[16,1024,256]{2,1,0:T(8,128)(2,1)} fusion(bf16[16,1024,256]{2,1,0:T(8,128)(2,1)} %bitcast.194, bf16[16,512,512]{2,1,0:T(8,128)(2,1)} %get-tuple-element.21, bf16[16,512,512]{2,1,0:T(8,128)(2,1)} %get-tuple-element.20, bf16[16,512,512]{2,1,0:T(8,128)(2,1)} %get-tuple-element.19), kind=kOutput, calls=%fused_computation.118 | convolution fusion | flops 8732540928 | bytes 41943040 | tf_op jit(solution)/shard_map/goq,gqk->gok/dot_general | solution.py:91
  685.1 16.4 %copy.55 = bf16[16,2,512,256]{3,1,0,2:T(2,128)(2,1)} copy(bf16[16,2,512,256]{3,2,1,0:T(8,128)(2,1)} %bitcast.193) | data formatting | bytes 16777216 | tf_op jit(solution)/shard_map/reshape | solution.py:95
  701.5 136.4 %all-to-all-done.4 = bf16[16,2,512,256]{3,1,0,2:T(2,128)(2,1)} async-done(((bf16[16,2,512,256]{3,1,0,2:T(2,128)(2,1)}), bf16[16,2,512,256]{3,1,0,2:T(2,128)(2,1)}, u32[]{:S(2)}, u32[]{:S(2)}) %all-to-all-start.4) | async-done | bytes 8388640 | tf_op jit(solution)/shard_map/all_to_all | solution.py:145
  838.0 5.6 all-to-all-start.3
  844.3 8.6 copy.49
  852.9 8.6 copy.46
  861.5 8.4 copy.72
  870.0 8.4 copy.52
  878.4 21.4 %multiply_convert_fusion = bf16[16,1024,256]{2,1,0:T(8,128)(2,1)} fusion(bf16[16,1024,256]{2,1,0:T(8,128)(2,1)} %bitcast.189, bf16[16,512,512]{2,1,0:T(8,128)(2,1)} %get-tuple-element.21, bf16[16,512,512]{2,1,0:T(8,128)(2,1)} %get-tuple-element.20, bf16[16,512,512]{2,1,0:T(8,128)(2,1)} %get-tuple-element.19), kind=kOutput, calls=%fused_computation.116 | convolution fusion | flops 8732540928 | bytes 41943040 | tf_op jit(solution)/shard_map/goq,gqk->gok/dot_general | solution.py:91
  899.8 16.6 %copy.65 = bf16[16,2,512,256]{3,1,0,2:T(2,128)(2,1)} copy(bf16[16,2,512,256]{3,2,1,0:T(8,128)(2,1)} %bitcast.190) | data formatting | bytes 16777216 | tf_op jit(solution)/shard_map/reshape | solution.py:95
  916.4 4.6 fusion.174
  921.0 2.3 fusion.173
  923.3 4.1 slice_bitcast_fusion.3
  927.4 4.0 slice_bitcast_fusion.5
  931.6 3.6 slice_bitcast_fusion.1
  935.2 91.0 %all-to-all-done.3 = bf16[16,2,512,256]{3,1,0,2:T(2,128)(2,1)} async-done(((bf16[16,2,512,256]{3,1,0,2:T(2,128)(2,1)}), bf16[16,2,512,256]{3,1,0,2:T(2,128)(2,1)}, u32[]{:S(2)}, u32[]{:S(2)}) %all-to-all-start.3) | async-done | bytes 8388640 | tf_op jit(solution)/shard_map/all_to_all | solution.py:145
  1026.3 5.8 all-to-all-start.5
  1032.1 4.4 fusion.175
  1036.5 23.4 %fusion.60 = f32[16,1024,512]{2,1,0:T(8,128)} fusion(bf16[16,512,256]{2,1,0:T(8,128)(2,1)} %fusion.173, bf16[16,512,256]{2,1,0:T(8,128)(2,1)} %get-tuple-element.18, bf16[16,512,256]{2,1,0:T(8,128)(2,1)} %get-tuple-element.17), kind=kOutput, calls=%fused_computation.92 | convolution fusion | flops 8673820672 | bytes 46137344 | tf_op jit(solution)/shard_map/cif,cjf->cij/dot_general | solution.py:85
  1059.9 22.4 %fusion.68 = f32[16,1024,512]{2,1,0:T(8,128)} fusion(bf16[16,512,256]{2,1,0:T(8,128)(2,1)S(1)} %copy-done.2, bf16[16,512,256]{2,1,0:T(8,128)(2,1)} %get-tuple-element.16, bf16[16,512,256]{2,1,0:T(8,128)(2,1)} %get-tuple-element.15), kind=kOutput, calls=%fused_computation.100 | convolution fusion | flops 8673820672 | bytes 46137344 | tf_op jit(solution)/shard_map/cif,cjf->cij/dot_general | solution.py:85
  1082.3 40.6 %add_multiply_fusion = f32[16,1024,512]{2,1,0:T(8,128)} fusion(f32[16,1024,512]{2,1,0:T(8,128)} %fusion.60, f32[16,1024,512]{2,1,0:T(8,128)} %fusion.68, bf16[16,512,256]{2,1,0:T(8,128)(2,1)} %fusion.175, bf16[16,512,256]{2,1,0:T(8,128)(2,1)} %get-tuple-element.14, bf16[16,512,256]{2,1,0:T(8,128)(2,1)} %get-tuple-element.13), kind=kOutput, calls=%fused_computation.1 | convolution fusion | flops 8698986496 | bytes 113246208 | tf_op jit(solution)/shard_map/cif,cjf->cij/dot_general | solution.py:85
  1123.0 11.6 copy.61
  1134.5 7.8 copy.62
  1142.3 19.6 %fusion.112 = bf16[128,256,128]{2,1,0:T(8,128)(2,1)S(1)} fusion(bf16[128,128,256]{2,1,0:T(8,128)(2,1)} %bitcast.185, s32[128]{0:T(128)S(1)} %copy-done.11, s32[128]{0:T(128)S(1)} %copy-done.9, pred[128]{0:T(512)(128)(4,1)S(1)} %copy-done.5, pred[128]{0:T(512)(128)(4,1)S(1)} %copy-done.7), kind=kOutput, calls=%fused_computation.148 | convolution fusion | flops 1078263808 | bytes 16778496 | tf_op jit(solution)/shard_map/oi,ibf->bfo/dot_general | solution.py:150
  1161.9 3.3 copy-done
  1165.3 4.8 collective-permute-start.2
  1170.1 11.6 copy.56
  1181.7 7.8 copy.57
  1189.4 19.4 %fusion.109 = bf16[128,256,128]{2,1,0:T(8,128)(2,1)S(1)} fusion(bf16[128,128,256]{2,1,0:T(8,128)(2,1)} %bitcast.187, s32[128]{0:T(128)S(1)} %copy-done.11, s32[128]{0:T(128)S(1)} %copy-done.9, pred[128]{0:T(512)(128)(4,1)S(1)} %copy-done.5, pred[128]{0:T(512)(128)(4,1)S(1)} %copy-done.7), kind=kOutput, calls=%fused_computation.147 | convolution fusion | flops 1078263808 | bytes 16778496 | tf_op jit(solution)/shard_map/oi,ibf->bfo/dot_general | solution.py:150
  1208.9 3.3 copy-done.1
  1212.2 2.3 collective-permute-start.1
  1214.6 11.8 convert_bitcast_fusion.2
  1226.4 11.5 copy.66
  1237.8 7.7 copy.67
  1245.6 22.7 %fusion.115 = bf16[128,256,128]{2,1,0:T(8,128)(2,1)} fusion(bf16[128,128,256]{2,1,0:T(8,128)(2,1)} %bitcast.183, s32[128]{0:T(128)S(1)} %copy-done.11, s32[128]{0:T(128)S(1)} %copy-done.9, pred[128]{0:T(512)(128)(4,1)S(1)} %copy-done.5, pred[128]{0:T(512)(128)(4,1)S(1)} %copy-done.7), kind=kOutput, calls=%fused_computation.149 | convolution fusion | flops 1078263808 | bytes 16778496 | tf_op jit(solution)/shard_map/oi,ibf->bfo/dot_general | solution.py:150
  1268.2 11.6 convert_bitcast_fusion
  1280.9 2.4 collective-permute-start.3
  1283.3 11.4 convert_bitcast_fusion.1
  1294.9 72.4 %fusion.108 = (bf16[1,128,256,128]{3,2,1,0:T(8,128)(2,1)}, bf16[1,128,256,128]{3,2,1,0:T(8,128)(2,1)}, bf16[1,128,256,128]{3,2,1,0:T(8,128)(2,1)}) fusion(f32[128,1,256,128]{3,2,0,1:T(8,128)} %convert_bitcast_fusion.2, f32[128,1,3,128]{3,2,0,1:T(4,128)S(1)} %convert_element_type.172, f32[128]{0:T(128)S(1)} %copy-done.15, f32[128]{0:T(128)S(1)} %copy-done.16, ...), kind=kLoop, calls=%fused_computation.146 | loop fusion | flops 150994944 | bytes 101255168 | tf_op jit(solution)/shard_map/transpose | solution.py:118
  1367.3 20.7 %pad_maximum_fusion = bf16[3,128,256,128]{3,2,1,0:T(8,128)(2,1)} fusion(bf16[1,128,256,128]{3,2,1,0:T(8,128)(2,1)} %get-tuple-element.27, bf16[1,128,256,128]{3,2,1,0:T(8,128)(2,1)} %get-tuple-element.26, bf16[1,128,256,128]{3,2,1,0:T(8,128)(2,1)} %get-tuple-element.25), kind=kLoop, calls=%fused_computation.5 | loop fusion | flops 25165824 | bytes 50331648 | tf_op jit(solution)/shard_map/concatenate | solution.py:156
  (76 shorter events, 3.2 us)
Async XLA Ops:
  2.0 28.5 %collective-permute-start = (bf16[3,128,3,128]{3,1,2,0:T(8,128)(2,1)S(1)}, bf16[3,128,3,128]{3,1,2,0:T(8,128)(2,1)S(1)}, u32[]{:S(2)}, u32[]{:S(2)}) collective-permute-start(bf16[3,128,3,128]{3,1,2,0:T(8,128)(2,1)S(1)} %copy.73), channel_id=1, source_target_pairs={{0,1},{1,8},{8,9},{9,16},{16,17},{17,24},{24,25},{2,3},{3,10},{10,... | collective-permute-start | bytes 884744 | tf_op jit(solution)/shard_map/ppermute | solution.py:18
  6.9 271.6 %copy-start.4 = (pred[128]{0:T(512)(128)(4,1)}, pred[128]{0:T(512)(128)(4,1)S(1)}, u32[]{:S(2)}) copy-start(pred[128]{0:T(512)(128)(4,1)S(1)} %get-tuple-element.38) | copy-start | bytes 388
  6.9 271.6 %copy-start.6 = (pred[128]{0:T(512)(128)(4,1)}, pred[128]{0:T(512)(128)(4,1)S(1)}, u32[]{:S(2)}) copy-start(pred[128]{0:T(512)(128)(4,1)S(1)} %get-tuple-element.39) | copy-start | bytes 388
  7.0 23.5 %copy-start.18 = (s32[128]{0:T(128)S(1)}, s32[128]{0:T(128)}, u32[]{:S(2)}) copy-start(s32[128]{0:T(128)} %param.6) | copy-start | bytes 1540
  7.0 23.4 %copy-start.12 = (f32[4,64]{1,0:T(4,128)S(1)}, f32[4,64]{1,0:T(4,128)}, u32[]{:S(2)}) copy-start(f32[4,64]{1,0:T(4,128)} %param.8) | copy-start | bytes 3076
  30.5 248.1 %copy-start.8 = (s32[128]{0:T(128)}, s32[128]{0:T(128)S(1)}, u32[]{:S(2)}) copy-start(s32[128]{0:T(128)S(1)} %get-tuple-element.36) | copy-start | bytes 1540
  30.5 248.1 %copy-start.10 = (s32[128]{0:T(128)}, s32[128]{0:T(128)S(1)}, u32[]{:S(2)}) copy-start(s32[128]{0:T(128)S(1)} %get-tuple-element.37) | copy-start | bytes 1540
  83.9 188.7 %all-to-all-start.2 = ((bf16[64,2,128,256]{3,1,2,0:T(2,128)(2,1)}), bf16[64,2,128,256]{3,1,2,0:T(2,128)(2,1)}, u32[]{:S(2)}, u32[]{:S(2)}) async-start(bf16[64,2,128,256]{3,1,2,0:T(2,128)(2,1)} %copy.51), calls=%async_computation.2 | async-start | bytes 16777216 | tf_op jit(solution)/shard_map/all_to_all | solution.py:140
  272.6 188.4 %all-to-all-start.1 = ((bf16[64,2,128,256]{3,1,2,0:T(2,128)(2,1)}), bf16[64,2,128,256]{3,1,2,0:T(2,128)(2,1)}, u32[]{:S(2)}, u32[]{:S(2)}) async-start(bf16[64,2,128,256]{3,1,2,0:T(2,128)(2,1)} %copy.48), calls=%async_computation.1 | async-start | bytes 16777216 | tf_op jit(solution)/shard_map/all_to_all | solution.py:140
  323.5 143.1 %copy-start.3 = (s32[512,512]{1,0:T(8,128)S(1)}, s32[512,512]{1,0:T(8,128)}, u32[]{:S(2)}) copy-start(s32[512,512]{1,0:T(8,128)} %param.7) | copy-start | bytes 3145732
  461.0 188.3 %all-to-all-start = ((bf16[64,2,128,256]{3,1,2,0:T(2,128)(2,1)}), bf16[64,2,128,256]{3,1,2,0:T(2,128)(2,1)}, u32[]{:S(2)}, u32[]{:S(2)}) async-start(bf16[64,2,128,256]{3,1,2,0:T(2,128)(2,1)} %copy.45), calls=%async_computation | async-start | bytes 16777216 | tf_op jit(solution)/shard_map/all_to_all | solution.py:140
  649.3 188.7 %all-to-all-start.4 = ((bf16[16,2,512,256]{3,1,0,2:T(2,128)(2,1)}), bf16[16,2,512,256]{3,1,0,2:T(2,128)(2,1)}, u32[]{:S(2)}, u32[]{:S(2)}) async-start(bf16[16,2,512,256]{3,1,0,2:T(2,128)(2,1)} %copy.60), calls=%async_computation.4 | async-start | bytes 16777216 | tf_op jit(solution)/shard_map/all_to_all | solution.py:145
  685.1 158.5 %copy-start.13 = (f32[4,64]{1,0:T(4,128)S(1)}, f32[4,64]{1,0:T(4,128)}, u32[]{:S(2)}) copy-start(f32[4,64]{1,0:T(4,128)} %param.9) | copy-start | bytes 3076
  838.0 188.3 %all-to-all-start.3 = ((bf16[16,2,512,256]{3,1,0,2:T(2,128)(2,1)}), bf16[16,2,512,256]{3,1,0,2:T(2,128)(2,1)}, u32[]{:S(2)}, u32[]{:S(2)}) async-start(bf16[16,2,512,256]{3,1,0,2:T(2,128)(2,1)} %copy.55), calls=%async_computation.3 | async-start | bytes 16777216 | tf_op jit(solution)/shard_map/all_to_all | solution.py:145
  899.8 21.3 %slice-start.2 = ((s8[8388608]{0:T(1024)(128)(4,1)}), s8[4194304]{0:T(1024)(128)(4,1)S(1)}, s32[]{:S(2)}) async-start(s8[8388608]{0:T(1024)(128)(4,1)} %bitcast.175), calls=%async_computation.8 | async-start | bytes 8388608
  899.8 21.3 %slice-start.3 = ((s8[8388608]{0:T(1024)(128)(4,1)}), s8[4194304]{0:T(1024)(128)(4,1)S(1)}, s32[]{:S(2)}) async-start(s8[8388608]{0:T(1024)(128)(4,1)} %bitcast.175), calls=%async_computation.9 | async-start | bytes 8388608
  899.8 23.5 %slice-start.4 = ((s8[8388608]{0:T(1024)(128)(4,1)}), s8[4194304]{0:T(1024)(128)(4,1)S(1)}, s32[]{:S(2)}) async-start(s8[8388608]{0:T(1024)(128)(4,1)} %bitcast.180), calls=%async_computation.10 | async-start | bytes 8388608
  916.4 6.9 slice-start.5
  923.3 8.1 slice-start
  927.4 4.2 slice-start.1
  1026.3 200.1 %all-to-all-start.5 = ((bf16[16,2,512,256]{3,1,0,2:T(2,128)(2,1)}), bf16[16,2,512,256]{3,1,0,2:T(2,128)(2,1)}, u32[]{:S(2)}, u32[]{:S(2)}) async-start(bf16[16,2,512,256]{3,1,0,2:T(2,128)(2,1)} %copy.65), calls=%async_computation.5 | async-start | bytes 16777216 | tf_op jit(solution)/shard_map/all_to_all | solution.py:145
  1036.5 23.4 %copy-start.2 = (bf16[16,512,256]{2,1,0:T(8,128)(2,1)S(1)}, bf16[16,512,256]{2,1,0:T(8,128)(2,1)}, u32[]{:S(2)}) copy-start(bf16[16,512,256]{2,1,0:T(8,128)(2,1)} %fusion.174) | copy-start | bytes 12582916
  1122.9 19.4 %copy-start.5 = (pred[128]{0:T(512)(128)(4,1)S(1)}, pred[128]{0:T(512)(128)(4,1)}, u32[]{:S(2)}) copy-start(pred[128]{0:T(512)(128)(4,1)} %copy-done.4) | copy-start | bytes 388
  1122.9 19.4 %copy-start.7 = (pred[128]{0:T(512)(128)(4,1)S(1)}, pred[128]{0:T(512)(128)(4,1)}, u32[]{:S(2)}) copy-start(pred[128]{0:T(512)(128)(4,1)} %copy-done.6) | copy-start | bytes 388
  1123.0 19.4 %copy-start.9 = (s32[128]{0:T(128)S(1)}, s32[128]{0:T(128)}, u32[]{:S(2)}) copy-start(s32[128]{0:T(128)} %copy-done.8) | copy-start | bytes 1540
  1123.0 19.4 %copy-start.11 = (s32[128]{0:T(128)S(1)}, s32[128]{0:T(128)}, u32[]{:S(2)}) copy-start(s32[128]{0:T(128)} %copy-done.10) | copy-start | bytes 1540
  1161.9 3.3 copy-start
  1165.3 129.4 %collective-permute-start.2 = (bf16[128,1,3,128]{3,2,0,1:T(4,128)(2,1)S(1)}, bf16[128,1,3,128]{3,2,0,1:T(4,128)(2,1)S(1)}, u32[]{:S(2)}, u32[]{:S(2)}) collective-permute-start(bf16[128,1,3,128]{3,2,0,1:T(4,128)(2,1)S(1)} %slice.216), channel_id=1, source_target_pairs={{0,1},{1,8},{8,9},{9,16},{16,17},{17,24},{24,25},{2,3},{3,10},{10,... | collective-permute-start | bytes 294920 | tf_op jit(solution)/shard_map/ppermute | solution.py:18
  1208.8 3.3 copy-start.1
  1212.2 82.5 %collective-permute-start.1 = (bf16[128,1,3,128]{3,2,0,1:T(4,128)(2,1)S(1)}, bf16[128,1,3,128]{3,2,0,1:T(4,128)(2,1)S(1)}, u32[]{:S(2)}, u32[]{:S(2)}) collective-permute-start(bf16[128,1,3,128]{3,2,0,1:T(4,128)(2,1)S(1)} %slice.211), channel_id=1, source_target_pairs={{0,1},{1,8},{8,9},{9,16},{16,17},{17,24},{24,25},{2,3},{3,10},{10,... | collective-permute-start | bytes 294920 | tf_op jit(solution)/shard_map/ppermute | solution.py:18
  1279.9 15.0 %copy-start.14 = (f32[128]{0:T(128)S(1)}, f32[128]{0:T(128)}, u32[]{:S(2)}) copy-start(f32[128]{0:T(128)} %get-tuple-element.28) | copy-start | bytes 1540
  1279.9 15.0 %copy-start.15 = (f32[128]{0:T(128)S(1)}, f32[128]{0:T(128)}, u32[]{:S(2)}) copy-start(f32[128]{0:T(128)} %get-tuple-element.29) | copy-start | bytes 1540
  1279.9 15.0 %copy-start.16 = (f32[128]{0:T(128)S(1)}, f32[128]{0:T(128)}, u32[]{:S(2)}) copy-start(f32[128]{0:T(128)} %get-tuple-element.30) | copy-start | bytes 1540
  1279.9 15.0 %copy-start.17 = (f32[128]{0:T(128)S(1)}, f32[128]{0:T(128)}, u32[]{:S(2)}) copy-start(f32[128]{0:T(128)} %get-tuple-element.31) | copy-start | bytes 1540
  1280.9 13.9 collective-permute-start.3
where the time goes:
time: 1400 us; the launch traced here: 1390 us
  waiting for transfers between devices  552 us (39%)
  matrix products  308 us (22%)
  local copies, waits for them, and re-layouts  245 us (18%)
  other arithmetic  233 us (17%)
  starting transfers between devices  49 us (4%)
    all_to_all x3, waiting for transfers between devices, per_device(): lax.all_to_all(spectra_list[batch_step], 'chan', split_axis=0, concat_axi...  325 us
    all_to_all x3, waiting for transfers between devices, per_device(): lax.all_to_all(form_beams(turned, steering_matrix), 'chan', split_axis=2,...  227 us
    dot_general x3, matrix products, channelize(): jnp.einsum('oi,afi->oaf', forward, weighted, preferred_element_type=jnp.f...  96.2 us
    dot_general x3, matrix products, gram_block(): jnp.einsum('cif,cjf->cij', stacked, left_part, preferred_element_type=jnp...  86.4 us
    transpose x1, other arithmetic, synthesize(): return jnp.transpose(weighted.astype(jnp.bfloat16), (1, 0, 2, 3))  72.4 us
    another operation x1, other arithmetic  70 us
    dot_general x3, matrix products, form_beams(): jnp.einsum('goq,gqk->gok', steering_matrix, flattened_rows, preferred_ele...  63.9 us
    reshape x6, local copies, waits for them, and re-layouts, channelize(): spectra.astype(jnp.bfloat16)  63.7 us
  transfers between devices with their start and end apart: 10, of which 5 were waited for; matrix products, arithmetic and copies ran while one was open for 45% of the time, Pallas kernels for 0%

commit v1 on v0

v1 whole, which is shorter than its diff:
```python
import math

import jax
import jax.numpy as jnp
from jax import lax
from jax.experimental import pallas as pl
from jax.experimental.pallas import tpu as pltpu
from jax.sharding import PartitionSpec as P


A = 512
C = 64
TAPS = 4
FB = 256
MB = 3
RIM = 8


def shifted(value, axis, steps):
    count = lax.axis_size(axis)
    leading, last = (max(0, -steps), min(count, count - steps))
    return lax.ppermute(value, axis, [(source, source + steps) for source in range(leading, last)])


def forward_table(chan_count):
    indices = jnp.arange(2 * chan_count, dtype=jnp.int32)
    out_chan = indices // 2
    out_part = indices % 2
    in_part = indices // chan_count
    in_sample = indices % chan_count
    wrapped = out_chan[:, None] * in_sample[None, :] % chan_count
    angles = wrapped.astype(jnp.float32) * (2.0 * math.pi / chan_count)
    cosine = jnp.cos(angles)
    sine_part = jnp.sin(angles)
    real_row = jnp.where(in_part[None, :] == 0, cosine, sine_part)
    imag_row = jnp.where(in_part[None, :] == 0, -sine_part, cosine)
    dft_table = jnp.where(out_part[:, None] == 0, real_row, imag_row)
    return (dft_table * (1.0 / math.sqrt(chan_count))).astype(jnp.bfloat16)


def inverse_table(chan_count):
    indices = jnp.arange(2 * chan_count, dtype=jnp.int32)
    out_part = indices // chan_count
    out_sample = indices % chan_count
    in_chan = indices // 2
    in_part = indices % 2
    wrapped = out_sample[:, None] * in_chan[None, :] % chan_count
    angles = wrapped.astype(jnp.float32) * (2.0 * math.pi / chan_count)
    cosine = jnp.cos(angles)
    sine_part = jnp.sin(angles)
    real_row = jnp.where(in_part[None, :] == 0, cosine, -sine_part)
    imag_row = jnp.where(in_part[None, :] == 0, sine_part, cosine)
    dft_table = jnp.where(out_part[:, None] == 0, real_row, imag_row)
    return (dft_table * (1.0 / math.sqrt(chan_count))).astype(jnp.bfloat16)


def steering_weights(delays, channel_list, chan_count):
    odd_steps = 2 * channel_list + 1
    wrapped = odd_steps[:, None, None] * delays[None, :, :] % (2 * chan_count)
    angles = wrapped.astype(jnp.float32) * (math.pi / chan_count)
    cosine = jnp.swapaxes(jnp.cos(angles), 1, 2)
    sine_part = jnp.swapaxes(jnp.sin(angles), 1, 2)
    upper = jnp.concatenate([cosine, sine_part], axis=2)
    lower = jnp.concatenate([-sine_part, cosine], axis=2)
    return jnp.concatenate([upper, lower], axis=1).astype(jnp.bfloat16)


def filtered(pad_ref, slot, taps, frames):
    total = taps[0:1] * pad_ref[slot, RIM : RIM + frames]
    for tap_number in range(1, TAPS):
        total = total + taps[tap_number : tap_number + 1] * pad_ref[
            slot, RIM - tap_number : RIM - tap_number + frames
        ]
    return total.astype(jnp.bfloat16)


def channelize_kernel(flags_ref, block_ref, rim_ref, taps_ref, forward_ref, out_ref, pad_ref):
    step = pl.program_id(0)
    groups, tile, rows, frames = out_ref.shape
    taps = taps_ref[...]
    forward = forward_ref[...]
    for slot in range(tile):
        pad_ref[slot, 0:RIM] = rim_ref[slot].astype(jnp.float32)
        pad_ref[slot, RIM : RIM + frames] = block_ref[0, slot].astype(jnp.float32)
        weighted = filtered(pad_ref, slot, taps, frames)
        spectra = lax.dot_general(
            forward, weighted, (((1,), (1,)), ((), ())), preferred_element_type=jnp.float32
        )
        scale = flags_ref[step * tile + slot].astype(jnp.float32)
        spectra = (spectra * scale).astype(jnp.bfloat16)
        out_ref[:, slot] = spectra.reshape(groups, rows, frames)


def channelize(voltages, batch_step, rim, taps, forward, flags, groups):
    antennas, frames, width = voltages.shape[1:]
    rows = width // groups
    tile = 8
    return pl.pallas_call(
        channelize_kernel,
        grid=(antennas // tile,),
        in_specs=[
            pl.BlockSpec(memory_space=pltpu.SMEM),
            pl.BlockSpec((1, tile, frames, width), lambda i: (batch_step, i, 0, 0)),
            pl.BlockSpec((tile, RIM, width), lambda i: (i, 0, 0)),
            pl.BlockSpec((TAPS, width), lambda i: (0, 0)),
            pl.BlockSpec((width, width), lambda i: (0, 0)),
        ],
        out_specs=pl.BlockSpec((groups, tile, rows, frames), lambda i: (0, i, 0, 0)),
        out_shape=jax.ShapeDtypeStruct((groups, antennas, rows, frames), jnp.bfloat16),
        scratch_shapes=[pltpu.VMEM((tile, RIM + frames, width), jnp.float32)],
        cost_estimate=pl.CostEstimate(
            flops=2 * antennas * frames * width * width,
            bytes_accessed=12 * antennas * frames * width,
            transcendentals=0,
        ),
        name="channelize",
    )(flags, voltages, rim, taps, forward)


def synthesize_kernel(*refs):
    piece_ref, tail_ref, taps_ref, inverse_ref = refs[:4]
    out_ref, pad_ref = refs[-2:]
    groups, tile, rows, frames = piece_ref.shape
    taps = taps_ref[...]
    inverse = inverse_ref[...]
    for slot in range(tile):
        block = piece_ref[:, slot].reshape(groups * rows, frames)
        result = lax.dot_general(
            block, inverse, (((0,), (1,)), ((), ())), preferred_element_type=jnp.float32
        )
        pad_ref[slot, 0:RIM] = tail_ref[slot].astype(jnp.float32)
        pad_ref[slot, RIM : RIM + frames] = result.astype(jnp.bfloat16).astype(jnp.float32)
        out_ref[0, slot] = filtered(pad_ref, slot, taps, frames)


def synthesize(piece, tails, taps, inverse_result, batch_step, held):
    groups, beams, rows, frames = piece.shape
    width = groups * rows
    tile = 8
    in_specs = [
        pl.BlockSpec((groups, tile, rows, frames), lambda i: (0, i, 0, 0)),
        pl.BlockSpec((tile, RIM, width), lambda i: (i, 0, 0)),
        pl.BlockSpec((TAPS, width), lambda i: (0, 0)),
        pl.BlockSpec((width, width), lambda i: (0, 0)),
    ]
    operands = [piece, tails, taps, inverse_result]
    aliases = {}
    if held is not None:
        in_specs.append(pl.BlockSpec(memory_space=pl.ANY))
        operands.append(held)
        aliases = {4: 0}
    return pl.pallas_call(
        synthesize_kernel,
        grid=(beams // tile,),
        in_specs=in_specs,
        out_specs=pl.BlockSpec((1, tile, frames, width), lambda i: (batch_step, i, 0, 0)),
        out_shape=jax.ShapeDtypeStruct((MB, beams, frames, width), jnp.bfloat16),
        scratch_shapes=[pltpu.VMEM((tile, RIM + frames, width), jnp.float32)],
        input_output_aliases=aliases,
        cost_estimate=pl.CostEstimate(
            flops=2 * beams * frames * width * width,
            bytes_accessed=12 * beams * frames * width,
            transcendentals=0,
        ),
        name="synthesize",
    )(*operands)


def gram_block(turned):
    left_part = jnp.concatenate([turned[:, 0], turned[:, 1]], axis=-1)
    rotated = jnp.concatenate([turned[:, 1], -turned[:, 0]], axis=-1)
    stacked = jnp.concatenate([left_part, rotated], axis=1)
    return jnp.einsum("cif,cjf->cij", stacked, left_part, preferred_element_type=jnp.float32)


def form_beams(turned, steering_matrix):
    chan_local, parts, antennas, frames = turned.shape
    flattened_rows = turned.reshape(chan_local, parts * antennas, frames)
    formed_beams = jnp.einsum(
        "goq,gqk->gok", steering_matrix, flattened_rows, preferred_element_type=jnp.float32
    )
    formed_beams = (formed_beams * (1.0 / math.sqrt(antennas))).astype(jnp.bfloat16)
    return formed_beams.reshape(chan_local, 2, steering_matrix.shape[1] // 2, frames)


def device_step(voltages, flags, delays, analysis_taps, synthesis_taps):
    groups = lax.axis_size("chan")
    chan_local = C // groups
    beam_local = delays.shape[1] // groups
    frames = voltages.shape[2]
    forward = forward_table(C)
    inverse_result = inverse_table(C)
    analysis_both = jnp.concatenate([analysis_taps, analysis_taps], axis=1)
    synthesis_both = jnp.concatenate([synthesis_taps, synthesis_taps], axis=1)
    channel_list = lax.axis_index("chan") * chan_local + jnp.arange(chan_local, dtype=jnp.int32)
    steering_matrix = steering_weights(delays, channel_list, C)
    spectra_list = []
    for batch_step in range(MB):
        rim = shifted(voltages[batch_step, :, frames - RIM :, :], ("segment", "tm"), 1)
        spectra_list.append(
            channelize(voltages, batch_step, rim, analysis_both, forward, flags, groups)
        )
    gram_total = None
    beams = None
    for batch_step in range(MB):
        arrived = lax.all_to_all(
            spectra_list[batch_step], "chan", split_axis=0, concat_axis=0, tiled=True
        )
        turned = jnp.transpose(
            arrived.reshape(groups, -1, chan_local, 2, frames), (2, 3, 0, 1, 4)
        ).reshape(chan_local, 2, -1, frames)
        gram_piece = gram_block(turned)
        gram_total = gram_piece if batch_step == 0 else gram_total + gram_piece
        formed = form_beams(turned, steering_matrix)
        outgoing = jnp.transpose(
            formed.reshape(chan_local, 2, groups, beam_local, frames), (2, 3, 0, 1, 4)
        ).reshape(groups, beam_local, 2 * chan_local, frames)
        piece = lax.all_to_all(outgoing, "chan", split_axis=0, concat_axis=0, tiled=True)
        last = jnp.einsum(
            "ogr,gbrf->bfo",
            inverse_result.reshape(2 * C, groups, 2 * chan_local),
            piece[:, :, :, frames - RIM :],
            preferred_element_type=jnp.float32,
        ).astype(jnp.bfloat16)
        tails = shifted(last, ("segment", "tm"), 1)
        beams = synthesize(piece, tails, synthesis_both, inverse_result, batch_step, beams)
    vis = (gram_total * (1.0 / (MB * FB))).reshape(chan_local, 1, 2, A, A)
    return (vis, beams)


def solution(mesh):
    placed = (P(None, "chan", ("segment", "tm"), None), P("chan"), P(), P(), P())
    return jax.shard_map(
        device_step,
        mesh=mesh,
        in_specs=placed,
        out_specs=(
            P("chan", ("segment", "tm"), None, None, None),
            P(None, "chan", ("segment", "tm"), None),
        ),
        check_vma=False,
    )
```

time: 1400 us -> 1270 us (0.907)
  other arithmetic: 233 us -> 80.8 us
  matrix products: 308 us -> 167 us
  Pallas kernels: 0 us -> 96.6 us
  waiting for transfers between devices: 552 us -> 642 us
  local copies, waits for them, and re-layouts: 245 us -> 219 us
    dot_general x6 -> x3, matrix products: 158 us -> 17.3 us  [device_step(): jnp.einsum('ogr,gbrf->bfo', inverse_result.reshape(2 * C, groups, 2 * cha...]
    all_to_all x12 -> x0, local copies, waits for them, and re-layouts: 109 us -> none  [the longest x6 57.9 us: per_device(): lax.all_to_all(form_beams(turned, steering_matrix), 'chan', split_axis=2,...]
    pallas_call x0 -> x6, Pallas kernels: none -> 96.6 us  [the longest x3 48.3 us: synthesize(): pl.pallas_call(synthesize_kernel, grid=(beams // tile,), in_specs=in_spec...]
    all_to_all x6, waiting for transfers between devices: 552 us -> 629 us  [the longest x3 354 us: device_step(): lax.all_to_all(spectra_list[batch_step], 'chan', split_axis=0, concat_axi...]
    transpose x1 -> x0, other arithmetic: 72.4 us -> none  [synthesize(): return jnp.transpose(weighted.astype(jnp.bfloat16), (1, 0, 2, 3))]
    transpose x0 -> x6, local copies, waits for them, and re-layouts: none -> 69.1 us  [device_step(): jnp.transpose(arrived.reshape(groups, -1, chan_local, 2, frames), (2, 3,...]
    convert_element_type x9 -> x1, other arithmetic: 58.4 us -> 1.23 us  [inverse_table(): return (dft_table * (1.0 / math.sqrt(chan_count))).astype(jnp.bfloat16)]
    another operation x0 -> x3, local copies, waits for them, and re-layouts: none -> 49.6 us  [device_step(): formed.reshape(chan_local, 2, groups, beam_local, frames)]
  transfers between devices with their start and end apart: 10 -> 12, of which waited for: 5 -> 9; matrix products, arithmetic and copies ran while one was open for 45% -> 36% of each run, Pallas kernels for 0% -> 5%
where the time goes in v1:
time: 1270 us; the launch traced here: 1260 us
  waiting for transfers between devices  642 us (51%)
  local copies, waits for them, and re-layouts  219 us (17%)
  matrix products  167 us (13%)
  Pallas kernels  96.6 us (8%)
  other arithmetic  80.8 us (6%)
  starting transfers between devices  53.9 us (4%)
    all_to_all x3, waiting for transfers between devices, device_step(): lax.all_to_all(spectra_list[batch_step], 'chan', split_axis=0, concat_axi...  354 us
    all_to_all x3, waiting for transfers between devices, device_step(): lax.all_to_all(outgoing, 'chan', split_axis=0, concat_axis=0, tiled=True)  276 us
    dot_general x3, matrix products, gram_block(): jnp.einsum('cif,cjf->cij', stacked, left_part, preferred_element_type=jnp...  86.3 us
    another operation x1, other arithmetic  70.1 us
    transpose x6, local copies, waits for them, and re-layouts, device_step(): jnp.transpose(arrived.reshape(groups, -1, chan_local, 2, frames), (2, 3,...  69.1 us
    dot_general x3, matrix products, form_beams(): jnp.einsum('goq,gqk->gok', steering_matrix, flattened_rows, preferred_ele...  63.9 us
    another operation x3, local copies, waits for them, and re-layouts, device_step(): formed.reshape(chan_local, 2, groups, beam_local, frames)  49.6 us
    pallas_call x3, Pallas kernels, synthesize(): pl.pallas_call(synthesize_kernel, grid=(beams // tile,), in_specs=in_spec...  48.3 us
  transfers between devices with their start and end apart: 12, of which 9 were waited for; matrix products, arithmetic and copies ran while one was open for 36% of the time, Pallas kernels for 5%

profile of v1, /device:TPU:0, one launch (start us, length us, event | category | flops | bytes accessed | tf_op | source)
XLA Modules:
  0.0 1260.6 jit_solution(8187900912012875606)
XLA Ops:
  0.6 1.2 slice_bitcast_fusion.6
  1.8 4.9 collective-permute-start
  6.7 1.4 pad_maximum_fusion.taps_ref
  8.1 1.2 multiply_convert_fusion.3
  9.4 2.9 collective-permute-done.rim_ref
  12.9 16.1 %channelize.3 = bf16[4,128,32,256]{3,2,1,0:T(8,128)(2,1)} custom-call(s32[128]{0:T(128)} %flags_ref.5, bf16[3,128,256,128]{3,2,1,0:T(8,128)(2,1)} %block_ref.5, bf16[128,8,128]{2,1,0:T(8,128)(2,1)} %copy-done.6, f32[4,128]{1,0:T(4,128)} %pad_maximum_fusion.taps_ref, bf16[128,128]{1,0:T(8,128)(2,1)} %get-tuple-element.17.forward_ref), custom_call_target="tpu_custom_call" | custom-call | flops 1073741824 | bytes 50331648 | tf_op jit(solution)/shard_map/channelize/pallas_call | solution.py:98
  29.0 5.6 all-to-all-start
  34.7 4.4 collective-permute-start.1
  39.1 4.7 collective-permute-done.1.rim_ref
  44.5 16.1 %channelize.4 = bf16[4,128,32,256]{3,2,1,0:T(8,128)(2,1)} custom-call(s32[128]{0:T(128)} %flags_ref.5, bf16[3,128,256,128]{3,2,1,0:T(8,128)(2,1)} %block_ref.5, bf16[128,8,128]{2,1,0:T(8,128)(2,1)} %copy-done.8, f32[4,128]{1,0:T(4,128)} %pad_maximum_fusion.taps_ref, bf16[128,128]{1,0:T(8,128)(2,1)} %get-tuple-element.17.forward_ref), custom_call_target="tpu_custom_call" | custom-call | flops 1073741824 | bytes 50331648 | tf_op jit(solution)/shard_map/channelize/pallas_call | solution.py:98
  60.6 158.2 %all-to-all-done = bf16[4,128,32,256]{3,2,1,0:T(8,128)(2,1)} async-done(((bf16[4,128,32,256]{3,2,1,0:T(8,128)(2,1)}), bf16[4,128,32,256]{3,2,1,0:T(8,128)(2,1)}, u32[]{:S(2)}, u32[]{:S(2)}) %all-to-all-start) | async-done | bytes 8388640 | tf_op jit(solution)/shard_map/all_to_all | solution.py:206
  218.7 5.7 all-to-all-start.1
  224.4 2.9 collective-permute-start.2
  227.3 4.7 collective-permute-done.2.rim_ref
  232.7 16.1 %channelize.5 = bf16[4,128,32,256]{3,2,1,0:T(8,128)(2,1)} custom-call(s32[128]{0:T(128)} %flags_ref.5, bf16[3,128,256,128]{3,2,1,0:T(8,128)(2,1)} %block_ref.5, bf16[128,8,128]{2,1,0:T(8,128)(2,1)} %copy-done.7, f32[4,128]{1,0:T(4,128)} %pad_maximum_fusion.taps_ref, bf16[128,128]{1,0:T(8,128)(2,1)} %get-tuple-element.17.forward_ref), custom_call_target="tpu_custom_call" | custom-call | flops 1073741824 | bytes 50331648 | tf_op jit(solution)/shard_map/channelize/pallas_call | solution.py:98
  248.8 158.8 %all-to-all-done.1 = bf16[4,128,32,256]{3,2,1,0:T(8,128)(2,1)} async-done(((bf16[4,128,32,256]{3,2,1,0:T(8,128)(2,1)}), bf16[4,128,32,256]{3,2,1,0:T(8,128)(2,1)}, u32[]{:S(2)}, u32[]{:S(2)}) %all-to-all-start.1) | async-done | bytes 8388640 | tf_op jit(solution)/shard_map/all_to_all | solution.py:206
  407.6 5.8 all-to-all-start.2
  413.8 70.1 %fusion.39 = (bf16[16,512,512]{2,1,0:T(8,128)(2,1)}, bf16[16,512,512]{2,1,0:T(8,128)(2,1)}, bf16[16,512,512]{2,1,0:T(8,128)(2,1)}) fusion(s32[512,512]{1,0:T(8,128)S(1)} %copy.12, s32[16]{0:T(128)S(1)} %multiply_add_fusion.1), kind=kLoop, calls=%fused_computation.52 | loop fusion | flops 75497472 | bytes 26214464 | tf_op jit(solution)/shard_map/convert.5
  483.9 13.1 %reshape.165 = bf16[4,128,16,2,256]{4,3,2,1,0:T(2,128)(2,1)} reshape(bf16[4,128,32,256]{3,2,1,0:T(8,128)(2,1)} %all-to-all-done) | data formatting | bytes 16777216 | tf_op jit(solution)/shard_map/reshape | solution.py:210
  496.9 11.6 copy.21
  508.5 21.3 %multiply_convert_fusion = bf16[16,1024,256]{2,1,0:T(8,128)(2,1)} fusion(bf16[16,1024,256]{2,1,0:T(8,128)(2,1)} %bitcast.104, bf16[16,512,512]{2,1,0:T(8,128)(2,1)} %get-tuple-element.15, bf16[16,512,512]{2,1,0:T(8,128)(2,1)} %get-tuple-element.14, bf16[16,512,512]{2,1,0:T(8,128)(2,1)} %get-tuple-element.13), kind=kOutput, calls=%fused_computation.34 | convolution fusion | flops 8732540928 | bytes 41943040 | tf_op jit(solution)/shard_map/goq,gqk->gok/dot_general | solution.py:179
  529.8 16.7 %copy.41 = bf16[16,2,4,128,256]{4,1,0,3,2:T(2,128)(2,1)} copy(bf16[16,2,4,128,256]{4,3,2,1,0:T(8,128)(2,1)} %bitcast.105) | data formatting | bytes 16777216 | tf_op jit(solution)/shard_map/reshape;reshape | solution.py:216
  546.4 13.1 %reshape.174 = bf16[4,128,32,256]{3,2,1,0:T(8,128)(2,1)} reshape(bf16[4,128,16,2,256]{4,3,2,1,0:T(2,128)(2,1)} %bitcast.99) | data formatting | bytes 16777216 | tf_op jit(solution)/shard_map/reshape | solution.py:217
  559.5 36.6 %all-to-all-done.2 = bf16[4,128,32,256]{3,2,1,0:T(8,128)(2,1)} async-done(((bf16[4,128,32,256]{3,2,1,0:T(8,128)(2,1)}), bf16[4,128,32,256]{3,2,1,0:T(8,128)(2,1)}, u32[]{:S(2)}, u32[]{:S(2)}) %all-to-all-start.2) | async-done | bytes 8388640 | tf_op jit(solution)/shard_map/all_to_all | solution.py:206
  596.1 5.6 all-to-all-start.5
  601.7 13.1 %reshape.167 = bf16[4,128,16,2,256]{4,3,2,1,0:T(2,128)(2,1)} reshape(bf16[4,128,32,256]{3,2,1,0:T(8,128)(2,1)} %all-to-all-done.1) | data formatting | bytes 16777216 | tf_op jit(solution)/shard_map/reshape | solution.py:210
  614.8 11.4 copy.17
  626.2 21.0 %multiply_convert_fusion.1 = bf16[16,1024,256]{2,1,0:T(8,128)(2,1)} fusion(bf16[16,1024,256]{2,1,0:T(8,128)(2,1)} %bitcast.107, bf16[16,512,512]{2,1,0:T(8,128)(2,1)} %get-tuple-element.15, bf16[16,512,512]{2,1,0:T(8,128)(2,1)} %get-tuple-element.14, bf16[16,512,512]{2,1,0:T(8,128)(2,1)} %get-tuple-element.13), kind=kOutput, calls=%fused_computation.35 | convolution fusion | flops 8732540928 | bytes 41943040 | tf_op jit(solution)/shard_map/goq,gqk->gok/dot_general | solution.py:179
  647.2 16.5 %copy.42 = bf16[16,2,4,128,256]{4,1,0,3,2:T(2,128)(2,1)} copy(bf16[16,2,4,128,256]{4,3,2,1,0:T(8,128)(2,1)} %bitcast.106) | data formatting | bytes 16777216 | tf_op jit(solution)/shard_map/reshape;reshape | solution.py:216
  663.7 13.1 %reshape.173 = bf16[4,128,32,256]{3,2,1,0:T(8,128)(2,1)} reshape(bf16[4,128,16,2,256]{4,3,2,1,0:T(2,128)(2,1)} %bitcast.100) | data formatting | bytes 16777216 | tf_op jit(solution)/shard_map/reshape | solution.py:217
  676.8 107.6 %all-to-all-done.5.refs_0_ = bf16[4,128,32,256]{3,2,1,0:T(8,128)(2,1)} async-done(((bf16[4,128,32,256]{3,2,1,0:T(8,128)(2,1)}), bf16[4,128,32,256]{3,2,1,0:T(8,128)(2,1)}, u32[]{:S(2)}, u32[]{:S(2)}) %all-to-all-start.5) | async-done | bytes 8388640 | tf_op jit(solution)/shard_map/all_to_all | solution.py:218
  784.4 6.1 all-to-all-start.4
  790.4 13.1 %reshape.169 = bf16[4,128,16,2,256]{4,3,2,1,0:T(2,128)(2,1)} reshape(bf16[4,128,32,256]{3,2,1,0:T(8,128)(2,1)} %all-to-all-done.2) | data formatting | bytes 16777216 | tf_op jit(solution)/shard_map/reshape | solution.py:210
  803.5 11.4 copy.13
  814.9 21.5 %multiply_convert_fusion.2 = bf16[16,1024,256]{2,1,0:T(8,128)(2,1)} fusion(bf16[16,1024,256]{2,1,0:T(8,128)(2,1)} %bitcast.103, bf16[16,512,512]{2,1,0:T(8,128)(2,1)} %get-tuple-element.15, bf16[16,512,512]{2,1,0:T(8,128)(2,1)} %get-tuple-element.14, bf16[16,512,512]{2,1,0:T(8,128)(2,1)} %get-tuple-element.13), kind=kOutput, calls=%fused_computation.36 | convolution fusion | flops 8732540928 | bytes 41943040 | tf_op jit(solution)/shard_map/goq,gqk->gok/dot_general | solution.py:179
  836.5 16.5 %copy.43 = bf16[16,2,4,128,256]{4,1,0,3,2:T(2,128)(2,1)} copy(bf16[16,2,4,128,256]{4,3,2,1,0:T(8,128)(2,1)} %bitcast.102) | data formatting | bytes 16777216 | tf_op jit(solution)/shard_map/reshape;reshape | solution.py:216
  853.0 13.1 %reshape.172 = bf16[4,128,32,256]{3,2,1,0:T(8,128)(2,1)} reshape(bf16[4,128,16,2,256]{4,3,2,1,0:T(2,128)(2,1)} %bitcast.101) | data formatting | bytes 16777216 | tf_op jit(solution)/shard_map/reshape | solution.py:217
  866.0 107.0 %all-to-all-done.4.refs_0_ = bf16[4,128,32,256]{3,2,1,0:T(8,128)(2,1)} async-done(((bf16[4,128,32,256]{3,2,1,0:T(8,128)(2,1)}), bf16[4,128,32,256]{3,2,1,0:T(8,128)(2,1)}, u32[]{:S(2)}, u32[]{:S(2)}) %all-to-all-start.4) | async-done | bytes 8388640 | tf_op jit(solution)/shard_map/all_to_all | solution.py:218
  973.1 5.8 all-to-all-start.3
  979.5 11.4 copy.10
  991.0 11.5 copy.9
  1002.5 11.8 copy.11
  1014.3 4.7 fusion.104
  1019.0 1.4 copy-done
  1020.7 0.9 slice-done
  1021.6 1.4 slice-done.1
  1023.1 2.4 fusion.105
  1025.5 1.5 copy-done.1
  1027.0 3.7 slice_bitcast_fusion.3
  1030.6 3.7 slice_bitcast_fusion.5
  1034.3 3.6 slice_bitcast_fusion.1
  1037.9 23.2 %fusion.11 = f32[16,1024,512]{2,1,0:T(8,128)} fusion(bf16[16,512,256]{2,1,0:T(8,128)(2,1)} %fusion.104, bf16[16,512,256]{2,1,0:T(8,128)(2,1)} %get-tuple-element.10, bf16[16,512,256]{2,1,0:T(8,128)(2,1)} %get-tuple-element.9), kind=kOutput, calls=%fused_computation.18 | convolution fusion | flops 8673820672 | bytes 46137344 | tf_op jit(solution)/shard_map/cif,cjf->cij/dot_general | solution.py:173
  1061.2 22.5 %fusion.3 = f32[16,1024,512]{2,1,0:T(8,128)} fusion(bf16[16,512,256]{2,1,0:T(8,128)(2,1)S(1)} %fusion.103, bf16[16,512,256]{2,1,0:T(8,128)(2,1)} %get-tuple-element.12, bf16[16,512,256]{2,1,0:T(8,128)(2,1)} %get-tuple-element.11), kind=kOutput, calls=%fused_computation.10 | convolution fusion | flops 8673820672 | bytes 46137344 | tf_op jit(solution)/shard_map/cif,cjf->cij/dot_general | solution.py:173
  1083.7 5.8 fusion.55
  1089.5 2.5 collective-permute-start.5
  1091.9 5.8 fusion.58
  1097.7 2.4 collective-permute-start.4
  1100.1 61.3 %all-to-all-done.3.refs_0_ = bf16[4,128,32,256]{3,2,1,0:T(8,128)(2,1)} async-done(((bf16[4,128,32,256]{3,2,1,0:T(8,128)(2,1)}), bf16[4,128,32,256]{3,2,1,0:T(8,128)(2,1)}, u32[]{:S(2)}, u32[]{:S(2)}) %all-to-all-start.3) | async-done | bytes 8388640 | tf_op jit(solution)/shard_map/all_to_all | solution.py:218
  1161.4 5.8 fusion.61
  1167.1 2.2 collective-permute-start.3
  1169.3 40.6 %add_multiply_fusion = f32[16,1024,512]{2,1,0:T(8,128)} fusion(f32[16,1024,512]{2,1,0:T(8,128)} %fusion.3, f32[16,1024,512]{2,1,0:T(8,128)} %fusion.11, bf16[16,512,256]{2,1,0:T(8,128)(2,1)} %fusion.105, bf16[16,512,256]{2,1,0:T(8,128)(2,1)} %get-tuple-element.8, bf16[16,512,256]{2,1,0:T(8,128)(2,1)} %get-tuple-element.7), kind=kOutput, calls=%fused_computation.1 | convolution fusion | flops 8698986496 | bytes 113246208 | tf_op jit(solution)/shard_map/cif,cjf->cij/dot_general | solution.py:173
  1210.6 16.1 %synthesize.3.refs_4_ = bf16[3,128,256,128]{3,2,1,0:T(8,128)(2,1)} custom-call(bf16[4,128,32,256]{3,2,1,0:T(8,128)(2,1)} %all-to-all-done.5.refs_0_, bf16[128,8,128]{2,1,0:T(8,128)(2,1)} %copy-done.4, f32[4,128]{1,0:T(4,128)} %pad_maximum_fusion.1.refs_2_, bf16[128,128]{1,0:T(8,128)(2,1)} %get-tuple-element.16.refs_3_), custom_call_target="tpu_custom_call" | custom-call | flops 1073741824 | bytes 50331648 | tf_op jit(solution)/shard_map/synthesize/pallas_call | solution.py:152
  1227.4 16.1 %synthesize.4.refs_4_ = bf16[3,128,256,128]{3,2,1,0:T(8,128)(2,1)} custom-call(bf16[4,128,32,256]{3,2,1,0:T(8,128)(2,1)} %all-to-all-done.4.refs_0_, bf16[128,8,128]{2,1,0:T(8,128)(2,1)} %copy-done.3, f32[4,128]{1,0:T(4,128)} %pad_maximum_fusion.1.refs_2_, bf16[128,128]{1,0:T(8,128)(2,1)} %get-tuple-element.16.refs_3_, ...), custom_call_target="tpu_custom_call", output_to_operand_aliasing={{}: (4, {})} | custom-call | flops 1073741824 | bytes 50331648 | tf_op jit(solution)/shard_map/synthesize/pallas_call | solution.py:152
  1244.2 16.1 %synthesize.5 = bf16[3,128,256,128]{3,2,1,0:T(8,128)(2,1)} custom-call(bf16[4,128,32,256]{3,2,1,0:T(8,128)(2,1)} %all-to-all-done.3.refs_0_, bf16[128,8,128]{2,1,0:T(8,128)(2,1)} %copy-done.5, f32[4,128]{1,0:T(4,128)} %pad_maximum_fusion.1.refs_2_, bf16[128,128]{1,0:T(8,128)(2,1)} %get-tuple-element.16.refs_3_, ...), custom_call_target="tpu_custom_call", output_to_operand_aliasing={{}: (4, {})} | custom-call | flops 1073741824 | bytes 50331648 | tf_op jit(solution)/shard_map/synthesize/pallas_call | solution.py:152
  (40 shorter events, 5.5 us)
Async XLA Ops:
  1.8 10.4 collective-permute-start
  6.7 5.5 copy-start.10
  8.1 4.1 copy-start.12
  12.2 0.7 copy-start.6
  29.0 189.7 %all-to-all-start = ((bf16[4,128,32,256]{3,2,1,0:T(8,128)(2,1)}), bf16[4,128,32,256]{3,2,1,0:T(8,128)(2,1)}, u32[]{:S(2)}, u32[]{:S(2)}) async-start(bf16[4,128,32,256]{3,2,1,0:T(8,128)(2,1)} %channelize.3), calls=%async_computation | async-start | bytes 16777216 | tf_op jit(solution)/shard_map/all_to_all | solution.py:206
  34.7 9.1 collective-permute-start.1
  43.8 0.7 copy-start.8
  218.7 188.9 %all-to-all-start.1 = ((bf16[4,128,32,256]{3,2,1,0:T(8,128)(2,1)}), bf16[4,128,32,256]{3,2,1,0:T(8,128)(2,1)}, u32[]{:S(2)}, u32[]{:S(2)}) async-start(bf16[4,128,32,256]{3,2,1,0:T(8,128)(2,1)} %channelize.4), calls=%async_computation.1 | async-start | bytes 16777216 | tf_op jit(solution)/shard_map/all_to_all | solution.py:206
  224.4 7.6 collective-permute-start.2
  232.0 0.7 copy-start.7
  248.8 164.6 %copy-start.2 = (s32[512,512]{1,0:T(8,128)S(1)}, s32[512,512]{1,0:T(8,128)}, u32[]{:S(2)}) copy-start(s32[512,512]{1,0:T(8,128)} %param.7) | copy-start | bytes 3145732
  407.6 188.5 %all-to-all-start.2 = ((bf16[4,128,32,256]{3,2,1,0:T(8,128)(2,1)}), bf16[4,128,32,256]{3,2,1,0:T(8,128)(2,1)}, u32[]{:S(2)}, u32[]{:S(2)}) async-start(bf16[4,128,32,256]{3,2,1,0:T(8,128)(2,1)} %channelize.5), calls=%async_computation.2 | async-start | bytes 16777216 | tf_op jit(solution)/shard_map/all_to_all | solution.py:206
  596.1 188.3 %all-to-all-start.5 = ((bf16[4,128,32,256]{3,2,1,0:T(8,128)(2,1)}), bf16[4,128,32,256]{3,2,1,0:T(8,128)(2,1)}, u32[]{:S(2)}, u32[]{:S(2)}) async-start(bf16[4,128,32,256]{3,2,1,0:T(8,128)(2,1)} %reshape.174), calls=%async_computation.5 | async-start | bytes 16777216 | tf_op jit(solution)/shard_map/all_to_all | solution.py:218
  784.4 188.7 %all-to-all-start.4 = ((bf16[4,128,32,256]{3,2,1,0:T(8,128)(2,1)}), bf16[4,128,32,256]{3,2,1,0:T(8,128)(2,1)}, u32[]{:S(2)}, u32[]{:S(2)}) async-start(bf16[4,128,32,256]{3,2,1,0:T(8,128)(2,1)} %reshape.173), calls=%async_computation.4 | async-start | bytes 16777216 | tf_op jit(solution)/shard_map/all_to_all | solution.py:218
  866.0 112.9 %copy-start.9 = (f32[4,64]{1,0:T(4,128)S(1)}, f32[4,64]{1,0:T(4,128)}, u32[]{:S(2)}) copy-start(f32[4,64]{1,0:T(4,128)} %param.9) | copy-start | bytes 3076
  973.1 188.3 %all-to-all-start.3 = ((bf16[4,128,32,256]{3,2,1,0:T(8,128)(2,1)}), bf16[4,128,32,256]{3,2,1,0:T(8,128)(2,1)}, u32[]{:S(2)}, u32[]{:S(2)}) async-start(bf16[4,128,32,256]{3,2,1,0:T(8,128)(2,1)} %reshape.172), calls=%async_computation.3 | async-start | bytes 16777216 | tf_op jit(solution)/shard_map/all_to_all | solution.py:218
  1014.3 6.2 copy-start
  1014.3 7.3 slice-start
  1020.4 2.6 slice-start.1
  1020.4 6.5 copy-start.1
  1061.1 22.6 %copy-start.11 = (s32[128]{0:T(128)S(1)}, s32[128]{0:T(128)}, u32[]{:S(2)}) copy-start(s32[128]{0:T(128)} %copy-done.10) | copy-start | bytes 1540
  1061.1 22.6 %copy-start.13 = (pred[128]{0:T(512)(128)(4,1)S(1)}, pred[128]{0:T(512)(128)(4,1)}, u32[]{:S(2)}) copy-start(pred[128]{0:T(512)(128)(4,1)} %copy-done.12) | copy-start | bytes 388
  1089.5 120.4 %collective-permute-start.5 = (bf16[128,8,128]{2,1,0:T(8,128)(2,1)S(1)}, bf16[128,8,128]{2,1,0:T(8,128)(2,1)S(1)}, u32[]{:S(2)}, u32[]{:S(2)}) collective-permute-start(bf16[128,8,128]{2,1,0:T(8,128)(2,1)S(1)} %fusion.55), channel_id=1, source_target_pairs={{0,1},{1,8},{8,9},{9,16},{16,17},{17,24},{24,25},{2,3},{3,10},{10,... | collective-permute-start | bytes 786440 | tf_op jit(solution)/shard_map/ppermute | solution.py:22
  1097.7 129.0 %collective-permute-start.4 = (bf16[128,8,128]{2,1,0:T(8,128)(2,1)S(1)}, bf16[128,8,128]{2,1,0:T(8,128)(2,1)S(1)}, u32[]{:S(2)}, u32[]{:S(2)}) collective-permute-start(bf16[128,8,128]{2,1,0:T(8,128)(2,1)S(1)} %fusion.58), channel_id=1, source_target_pairs={{0,1},{1,8},{8,9},{9,16},{16,17},{17,24},{24,25},{2,3},{3,10},{10,... | collective-permute-start | bytes 786440 | tf_op jit(solution)/shard_map/ppermute | solution.py:22
  1167.1 76.4 %collective-permute-start.3 = (bf16[128,8,128]{2,1,0:T(8,128)(2,1)S(1)}, bf16[128,8,128]{2,1,0:T(8,128)(2,1)S(1)}, u32[]{:S(2)}, u32[]{:S(2)}) collective-permute-start(bf16[128,8,128]{2,1,0:T(8,128)(2,1)S(1)} %fusion.61), channel_id=1, source_target_pairs={{0,1},{1,8},{8,9},{9,16},{16,17},{17,24},{24,25},{2,3},{3,10},{10,... | collective-permute-start | bytes 786440 | tf_op jit(solution)/shard_map/ppermute | solution.py:22
  1209.9 0.7 copy-start.4
  1226.7 0.7 copy-start.3
  1243.5 0.7 copy-start.5
